TPU v7x, 32 devices: a whole 2x2x4 slice. The times are simulated.
32 devices in a mesh: pairs: 8 (over z, x), grp: 4 (over y, core).
Axes of the slice: x: 2, y: 2, z: 4, core: 2. Of those that a mesh axis runs over, the one named last changes fastest.
Arguments:
- coefficients: bfloat16 [128, 512, 128], P('pairs', 'grp'), may hold values from -0.4140625 to 0.4140625
- domain: int32 [128, 512], P('pairs', 'grp'), may hold values from 0 to 767, as said below
- coupling_owner: int32 [128, 8], P('pairs'), may hold values from 0 to 7, all different within a row; in each aligned block of 16 rows (0 to 15, 16 to 31, ...) at most 16 rows name the same one
- coupling_slot: int32 [128, 8], P('pairs'), may hold values from 0 to 15
- coupling_fock: float32 [128, 8], P('pairs'), may hold values from -0.5 to 0.5
- exchange_integrals: float32 [128, 128, 128], P('pairs'), may hold values from -6 to 6
- pno_energy: float32 [128, 128], P('pairs'), may hold values from 0.3 to 3
- pair_shift: float32 [128], P('pairs'), may hold values from 0.4 to 2
- amplitudes_start: float32 [128, 128, 128], P('pairs'), may hold values from -1.8 to 1.8
Outputs:
- amplitudes: float32 [128, 128, 128], P('pairs')
Inputs may be any that keep to these rules, and one draw needn't show every extreme that they name: `coupling_owner`: each row names different indices. Among the 16 rows of one index of pairs no value is named more than 16 times, a bound that some block reaches. `domain`: for each pair and each g from 0 to 3, the entries g * 128 to (g + 1) * 128 - 1 are distinct numbers from g * 192 to (g + 1) * 192 - 1.
All inputs are finite; a program needn't handle non-finite values.
Results may differ from a plain program's by a relative error of at most 0.0025.
Values may be sent and summed in bfloat16 or wider, within the bound.
A program may use at most 128 MiB of HBM per device.

v0:
```python
import jax
import jax.numpy as jnp
from jax import lax
from jax.sharding import PartitionSpec as P

NB = 192
ITERS = 2


def on_device(
    coefficients,
    domain,
    coupling_owner,
    coupling_slot,
    coupling_fock,
    exchange_integrals,
    pno_energy,
    pair_shift,
    amplitudes_start,
):
    pair_count = coefficients.shape[0]
    block_rows = coefficients.shape[1]
    pno_count = coefficients.shape[2]
    link_count = coupling_owner.shape[1]
    pair_ranks = lax.axis_size("pairs")
    capacity = min(pair_count, (pair_count * link_count + pair_ranks - 1) // pair_ranks + 1)
    group_index = lax.axis_index("grp")
    local_dom = domain - group_index * NB
    owners = coupling_owner.T.reshape(-1)
    slots = coupling_slot.T.reshape(-1)
    owner_hits = (owners[:, None] == jnp.arange(pair_ranks, dtype=jnp.int32)[None, :]).astype(
        jnp.int32
    )
    earlier = jnp.cumsum(owner_hits, axis=0) - owner_hits
    link_rank = jnp.sum(earlier * owner_hits, axis=1)
    slot_hits = owner_hits[:, :, None] * (
        link_rank[:, None, None] == jnp.arange(capacity, dtype=jnp.int32)[None, None, :]
    ).astype(jnp.int32)
    request = jnp.sum(slot_hits * slots[:, None, None], axis=0)
    wanted = lax.all_to_all(request, "pairs", split_axis=0, concat_axis=0, tiled=True).reshape(-1)
    position = owners * capacity + link_rank
    outgoing_rows = jnp.take(coefficients, wanted, axis=0).reshape(
        pair_ranks, capacity, block_rows, pno_count
    )
    outgoing_dom = jnp.take(local_dom, wanted, axis=0).reshape(pair_ranks, capacity, block_rows)
    incoming_rows = lax.all_to_all(outgoing_rows, "pairs", split_axis=0, concat_axis=0, tiled=True)
    incoming_dom = lax.all_to_all(outgoing_dom, "pairs", split_axis=0, concat_axis=0, tiled=True)
    source_rows = jnp.take(
        incoming_rows.reshape(pair_ranks * capacity, block_rows, pno_count), position, axis=0
    )
    source_rows = source_rows.reshape(link_count, pair_count, block_rows, pno_count)
    source_dom = jnp.take(incoming_dom.reshape(pair_ranks * capacity, block_rows), position, axis=0)
    source_dom = source_dom.reshape(link_count, pair_count, block_rows)
    match = (local_dom[None, :, :, None] == source_dom[:, :, None, :]).astype(jnp.bfloat16)
    gathered = jnp.einsum(
        "kprs,kpsc->kprc", match, source_rows, preferred_element_type=jnp.float32
    ).astype(jnp.bfloat16)
    position_links = position.reshape(link_count, pair_count)
    fock_links = coupling_fock.T
    intersection = lax.psum(
        jnp.einsum("pra,kprc->kpac", coefficients, gathered, preferred_element_type=jnp.float32),
        "grp",
    )
    intersection_half = intersection.astype(jnp.bfloat16)
    used_links = intersection_half.shape[0]
    denominator = pno_energy[:, :, None] + pno_energy[:, None, :] + pair_shift[:, None, None]
    amplitudes = amplitudes_start
    for iteration in range(ITERS):
        sendable = amplitudes.astype(jnp.bfloat16)
        outgoing_amp = jnp.take(sendable, wanted, axis=0).reshape(
            pair_ranks, capacity, pno_count, pno_count
        )
        incoming_amp = lax.all_to_all(
            outgoing_amp, "pairs", split_axis=0, concat_axis=0, tiled=True
        )
        source_amp = jnp.take(
            incoming_amp.reshape(pair_ranks * capacity, pno_count, pno_count),
            position_links.reshape(-1),
            axis=0,
        )
        source_amp = source_amp.reshape(used_links, pair_count, pno_count, pno_count)
        half_proj = jnp.einsum(
            "kpac,kpcd->kpad", intersection_half, source_amp, preferred_element_type=jnp.float32
        ).astype(jnp.bfloat16)
        projected = jnp.einsum(
            "kpad,kpbd->kpab", half_proj, intersection_half, preferred_element_type=jnp.float32
        )
        coupled = jnp.sum(fock_links[:, :, None, None] * projected, axis=0)
        amplitudes = -(exchange_integrals + coupled) / denominator
    return amplitudes


def solution(mesh):
    placed = (
        P("pairs", "grp", None),
        P("pairs", "grp"),
        P("pairs", None),
        P("pairs", None),
        P("pairs", None),
        P("pairs", None, None),
        P("pairs", None),
        P("pairs"),
        P("pairs", None, None),
    )
    return jax.shard_map(
        on_device, mesh=mesh, in_specs=placed, out_specs=P("pairs", None, None), check_vma=False
    )
```

profile of v0, /device:TPU:0, one launch (start us, length us, event | category | flops | bytes accessed | tf_op | source)
XLA Modules:
  0.0 524.1 jit_solution(13798727091787789117)
XLA Ops:
  0.0 0.8 reshape.197
  0.8 0.8 mul.76
  2.1 0.8 multiply_reduce_fusion.2
  2.9 7.3 %all-to-all-start = ((s32[8,1,16]{2,1,0:T(1,128)}), s32[8,1,16]{2,1,0:T(1,128)S(1)}, u32[]{:S(2)}, u32[]{:S(2)}) async-start(s32[8,1,16]{2,1,0:T(1,128)} %bitcast.4), calls=%async_computation | async-start | bytes 8192 | tf_op jit(solution)/shard_map/all_to_all | solution.py:40
  10.2 0.7 broadcast_subtract_fusion
  10.9 1.3 convert_element_type.38
  12.2 4.4 all-to-all-done
  16.8 0.5 broadcast.152
  17.3 0.7 reduce.5
  18.0 0.6 gather_fusion
  18.7 0.7 broadcast_select_fusion.7
  19.4 3.4 all-to-all-start.1
  22.8 3.0 gather_fusion.4
  25.8 3.1 gather_fusion.2
  28.8 6.0 %broadcast_select_fusion.3 = (bf16[128,128,128]{2,1,0:T(8,128)(2,1)}, bf16[128,128,128]{2,1,0:T(8,128)(2,1)}) fusion(bf16[128,128,128]{2,1,0:T(8,128)(2,1)} %gather_fusion.4, pred[128]{0:T(512)(128)(4,1)S(1)} %compare_and_fusion.3, bf16[128,128,128]{2,1,0:T(8,128)(2,1)} %gather_fusion.2), kind=kLoop, calls=%fused_computation.24 | loop fusion | flops 4194304 | bytes 16777344 | tf_op jit(solution)/shard_map/jit(_take)/select_n | solution.py:70
  34.8 97.5 %all_to_all.29 = bf16[8,16,128,128]{3,2,1,0:T(8,128)(2,1)} all-to-all(bf16[8,16,128,128]{3,2,1,0:T(8,128)(2,1)} %bitcast.41), channel_id=1, replica_groups=mesh['pairs'=8,'grp'=4] {'pairs'}, dimensions={0} | all-to-all | bytes 8388608 | tf_op jit(solution)/shard_map/all_to_all | solution.py:46
  132.3 4.7 all-to-all-start.3
  137.2 0.6 gather_fusion.1
  138.0 5.2 gather_fusion.3
  143.2 85.8 %all-to-all-done.3 = bf16[8,16,128,128]{3,2,1,0:T(8,128)(2,1)} async-done(((bf16[8,16,128,128]{3,2,1,0:T(8,128)(2,1)}), bf16[8,16,128,128]{3,2,1,0:T(8,128)(2,1)}, u32[]{:S(2)}, u32[]{:S(2)}) %all-to-all-start.3) | async-done | bytes 4194336 | tf_op jit(solution)/shard_map/all_to_all | solution.py:73
  229.1 5.2 %gather_fusion.5 = bf16[128,128,128]{2,1,0:T(8,128)(2,1)} fusion(bf16[128,128,128]{2,1,0:T(8,128)(2,1)} %bitcast.19, s32[1024]{0:T(1024)S(1)} %pad_clamp_fusion), kind=kCustom, calls=%fused_computation.4.clone | custom fusion | bytes 8389120 | tf_op jit(solution)/shard_map/jit(_take)/gather | solution.py:76
  234.3 6.0 %broadcast_select_fusion = (bf16[128,128,128]{2,1,0:T(8,128)(2,1)}, bf16[128,128,128]{2,1,0:T(8,128)(2,1)}) fusion(bf16[128,128,128]{2,1,0:T(8,128)(2,1)} %gather_fusion.5, pred[128]{0:T(512)(128)(4,1)S(1)} %get-tuple-element.6, bf16[128,128,128]{2,1,0:T(8,128)(2,1)} %gather_fusion.3), kind=kLoop, calls=%fused_computation.21 | loop fusion | flops 4194304 | bytes 16777344 | tf_op jit(solution)/shard_map/jit(_take)/select_n | solution.py:76
  240.3 6.5 %fusion.11 = f32[8,16,128,128]{2,3,0,1:T(8,128)} fusion(bf16[8,16,128,128]{3,2,1,0:T(8,128)(2,1)} %bitcast.43, s32[8,16,128]{2,0,1:T(8,128)S(1)} %copy.25, s32[16,128]{1,0:T(8,128)S(1)} %broadcast_subtract_fusion, bf16[16,128,128]{2,1,0:T(8,128)(2,1)S(1)} %copy-done), kind=kOutput, calls=%fused_computation.27 | convolution fusion | flops 1077936128 | bytes 13180928 | tf_op jit(solution)/shard_map/pra,kprc->kpac/dot_general | solution.py:61
  246.8 146.3 %all-reduce.1 = bf16[8,16,128,128]{2,3,0,1:T(8,128)(2,1)} all-reduce(f32[8,16,128,128]{2,3,0,1:T(8,128)} %fusion.11), channel_id=1, replica_groups=mesh['pairs'=8,'grp'=4] {'grp'}, use_global_device_ids=true, to_apply=%region_3.6 | all-reduce | flops 2097152 | bytes 12582912 | tf_op jit(solution)/shard_map/psum | solution.py:60
  393.1 7.5 %multiply_reduce_fusion.1 = f32[16,128,128]{2,1,0:T(8,128)S(1)} fusion(f32[8,16]{1,0:T(8,128)S(1)} %bitcast.55, bf16[8,16,128,128]{2,3,0,1:T(8,128)(2,1)} %all-reduce.1, bf16[8,16,128,128]{3,2,1,0:T(8,128)(2,1)} %bitcast.47), kind=kOutput, calls=%fused_computation.9 | convolution fusion | flops 1079771136 | bytes 9437696 | tf_op jit(solution)/shard_map/kpad,kpbd->kpab/dot_general | solution.py:85
  401.1 3.0 gather_fusion.6
  404.1 2.6 broadcast_select_fusion.4
  406.7 98.6 %all_to_all.30 = bf16[8,16,128,128]{3,2,1,0:T(8,128)(2,1)} all-to-all(bf16[8,16,128,128]{3,2,1,0:T(8,128)(2,1)S(1)} %bitcast.44), channel_id=1, replica_groups=mesh['pairs'=8,'grp'=4] {'pairs'}, dimensions={0} | all-to-all | bytes 8388608 | tf_op jit(solution)/shard_map/all_to_all | solution.py:73
  505.4 5.2 %gather_fusion.7 = bf16[128,128,128]{2,1,0:T(8,128)(2,1)} fusion(bf16[128,128,128]{2,1,0:T(8,128)(2,1)} %bitcast.45, s32[1024]{0:T(1024)S(1)} %pad_clamp_fusion), kind=kCustom, calls=%fused_computation.5.clone | custom fusion | bytes 8389120 | tf_op jit(solution)/shard_map/jit(_take)/gather | solution.py:76
  510.6 4.6 broadcast_select_fusion.1
  515.2 7.5 %multiply_reduce_fusion = f32[16,128,128]{2,1,0:T(8,128)S(1)} fusion(f32[8,16]{1,0:T(8,128)S(1)} %bitcast.56, bf16[8,16,128,128]{2,3,0,1:T(8,128)(2,1)} %all-reduce.1, bf16[8,16,128,128]{3,2,1,0:T(8,128)(2,1)} %bitcast.48), kind=kOutput, calls=%fused_computation.8 | convolution fusion | flops 1079771136 | bytes 9437696 | tf_op jit(solution)/shard_map/kpad,kpbd->kpab/dot_general | solution.py:85
  522.7 1.4 negate_divide_fusion
  (39 shorter events, 1.4 us)
Async XLA Ops:
  0.0 25.8 %copy-start = (bf16[16,128,128]{2,1,0:T(8,128)(2,1)S(1)}, bf16[16,128,128]{2,1,0:T(8,128)(2,1)}, u32[]{:S(2)}) copy-start(bf16[16,128,128]{2,1,0:T(8,128)(2,1)} %param.13) | copy-start | bytes 1572868
  2.9 13.7 %all-to-all-start = ((s32[8,1,16]{2,1,0:T(1,128)}), s32[8,1,16]{2,1,0:T(1,128)S(1)}, u32[]{:S(2)}, u32[]{:S(2)}) async-start(s32[8,1,16]{2,1,0:T(1,128)} %bitcast.4), calls=%async_computation | async-start | bytes 8192 | tf_op jit(solution)/shard_map/all_to_all | solution.py:40
  19.4 15.4 %all-to-all-start.1 = ((s32[8,16,128]{2,1,0:T(8,128)}), s32[8,16,128]{2,1,0:T(8,128)S(1)}, u32[]{:S(2)}, u32[]{:S(2)}) async-start(s32[8,16,128]{2,1,0:T(8,128)} %broadcast_select_fusion.7), calls=%async_computation.1 | async-start | bytes 131072 | tf_op jit(solution)/shard_map/all_to_all | solution.py:47
  132.3 4.8 copy-start.4
  132.3 96.7 %all-to-all-start.3 = ((bf16[8,16,128,128]{3,2,1,0:T(8,128)(2,1)}), bf16[8,16,128,128]{3,2,1,0:T(8,128)(2,1)}, u32[]{:S(2)}, u32[]{:S(2)}) async-start(bf16[8,16,128,128]{3,2,1,0:T(8,128)(2,1)} %bitcast.40), calls=%async_computation.3 | async-start | bytes 8388608 | tf_op jit(solution)/shard_map/all_to_all | solution.py:73
  246.8 146.3 %copy-start.6 = (f32[16,8]{0,1:T(8,128)S(1)}, f32[16,8]{0,1:T(8,128)}, u32[]{:S(2)}) copy-start(f32[16,8]{0,1:T(8,128)} %param.17) | copy-start | bytes 1540
  393.1 7.5 %copy-start.2 = (f32[16,128,128]{2,1,0:T(8,128)S(1)}, f32[16,128,128]{2,1,0:T(8,128)}, u32[]{:S(2)}) copy-start(f32[16,128,128]{2,1,0:T(8,128)} %param.18) | copy-start | bytes 3145732
  393.1 7.5 %copy-start.3 = (f32[16,128]{1,0:T(8,128)S(1)}, f32[16,128]{1,0:T(8,128)}, u32[]{:S(2)}) copy-start(f32[16,128]{1,0:T(8,128)} %param.19) | copy-start | bytes 24580
  393.1 7.5 %copy-start.5 = (f32[16]{0:T(128)S(1)}, f32[16]{0:T(128)}, u32[]{:S(2)}) copy-start(f32[16]{0:T(128)} %param.20) | copy-start | bytes 196
  515.2 8.9 %copy-start.1 = (bf16[16,128,128]{2,1,0:T(8,128)(2,1)S(1)}, bf16[16,128,128]{2,1,0:T(8,128)(2,1)}, u32[]{:S(2)}) copy-start(bf16[16,128,128]{2,1,0:T(8,128)(2,1)} %param.13) | copy-start | bytes 1572868
where the time goes:
time: 525 us; the launch traced here: 524 us
  blocking collectives  342 us (65%)
  waiting for transfers between devices  90.2 us (17%)
  local copies, waits for them, and re-layouts  28.6 us (5%)
  other arithmetic  25.8 us (5%)
  matrix products  21.5 us (4%)
  starting transfers between devices  15.3 us (3%)
    psum x1, blocking collectives, on_device(): lax.psum(jnp.einsum('pra,kprc->kpac', coefficients, gathered, preferred_e...  146 us
    all_to_all x1, blocking collectives, on_device(): lax.all_to_all(outgoing_amp, 'pairs', split_axis=0, concat_axis=0, tiled=...  98.6 us
    all_to_all x1, blocking collectives, on_device(): lax.all_to_all(outgoing_rows, 'pairs', split_axis=0, concat_axis=0, tiled...  97.5 us
    all_to_all x1, waiting for transfers between devices, on_device(): lax.all_to_all(outgoing_amp, 'pairs', split_axis=0, concat_axis=0, tiled=...  85.8 us
    dot_general x2, matrix products, on_device(): jnp.einsum('kpad,kpbd->kpab', half_proj, intersection_half, preferred_ele...  15 us
    select_n x2, other arithmetic, on_device(): jnp.take(incoming_amp.reshape(pair_ranks * capacity, pno_count, pno_count...  10.6 us
  transfers between devices with their start and end apart: 3, of which 2 were waited for; matrix products, arithmetic and copies ran while one was open for 4% of the time, Pallas kernels for 0%

commit v1 on v0

v1 whole, which is shorter than its diff:
```python
import functools

import jax
import jax.numpy as jnp
from jax import lax
from jax.experimental import pallas as pl
from jax.experimental.pallas import tpu as pltpu
from jax.sharding import PartitionSpec as P

NB = 192
MESH = pl.DeviceIdType.MESH
F32, BF16 = jnp.float32, jnp.bfloat16


def ring_position(rank, n):
    odd = rank % 2
    return (1 - odd) * (rank // 2) + odd * (n - 1 - rank // 2)


def ring_rank(position, n):
    back = position // (n // 2)
    return (1 - back) * 2 * position + back * (2 * (n - 1 - position) + 1)


def places(n):
    p, g = lax.axis_index("pairs"), lax.axis_index("grp")
    position = ring_position(p, n)
    core, half = g % 2, g // 2
    mate = 2 * half + (1 - core)
    across = 2 * (1 - half) + core
    return p, g, position, mate, across


def at(position, n):
    return ring_rank((position + n) % n, n)


def greet(peers):
    barrier = pltpu.get_barrier_semaphore()
    for peer in peers:
        pl.semaphore_signal(barrier, inc=1, device_id=peer, device_id_type=MESH)
    pl.semaphore_wait(barrier, len(peers))


def remote(src, dst, send, recv, peer):
    return pltpu.make_async_remote_copy(
        src_ref=src, dst_ref=dst, send_sem=send, recv_sem=recv, device_id=peer, device_id_type=MESH
    )


def ring_parts(steps, parts):
    def of(step, direction):
        if step < steps:
            return tuple(range(parts))
        return tuple(c for c in range(parts) if c % 2 == direction)

    return of


def intersections(
    n, slot_ref, c_ref, dom_ref, out_ref,
    cbuf, dbuf, turned, wide, own, msend, mrecv, ysend, yrecv, keep,
    rs, rr, ms, mr, ys, yr,
):
    p, g, position, mate, across = places(n)
    pc = c_ref.shape[0]
    quarter = pc // 4
    rows = c_ref.shape[1]
    steps = n // 2
    right, left = at(position + 1, n), at(position - 1, n)
    ring_peer = (lambda r: (r, g))
    peers = [(right, g), (left, g), (p, mate), (p, across)]
    greet(peers)
    parts_of = ring_parts(steps, 3)
    hp = pc // 2

    def part(ref_c, ref_d, c):
        if c == 2:
            return ref_d
        return ref_c.at[pl.ds(c * hp, hp)]

    def move(step, direction, c):
        offset = -(step - 1) if direction == 0 else step - 1
        rank = at(position + offset, n)
        if step == 1:
            src = part(c_ref, dom_ref, c)
        else:
            src = part(cbuf.at[rank], dbuf.at[rank], c)
        dst = part(cbuf.at[rank], dbuf.at[rank], c)
        return remote(
            src, dst, rs.at[direction, step - 1, c], rr.at[direction, step - 1, c],
            ring_peer(right if direction == 0 else left),
        )

    def arrive(step, direction, c):
        offset = -step if direction == 0 else step
        rank = at(position + offset, n)
        dst = part(cbuf.at[rank], dbuf.at[rank], c)
        remote(
            dst, dst, rs.at[direction, step - 1, c], rr.at[direction, step - 1, c],
            ring_peer(left if direction == 0 else right),
        ).wait_recv()

    for c in (2, 0, 1):
        for d in (0, 1):
            if c in parts_of(1, d):
                move(1, d, c).start()

    base = g * NB
    lines = lax.broadcasted_iota(jnp.int32, (NB, rows), 0)
    core, half = g % 2, g // 2

    def expand(block, doms):
        def one(s, carry):
            hit = (lines == (doms[pl.ds(s, 1), :] - base)).astype(F32).astype(BF16)
            wide[s] = jnp.dot(hit, block[s], preferred_element_type=F32).astype(BF16)
            return carry

        lax.fori_loop(0, pc, one, 0, unroll=8)

    def mate_copy(k, rank):
        return remote(msend.at[k % 2], mrecv.at[rank], ms.at[k], mr.at[k], (p, mate))

    def across_copy(k, rank):
        return remote(ysend.at[k % 2], yrecv.at[rank], ys.at[k], yr.at[k], (p, across))

    ranks = []

    def product(t, rank):
        return jnp.dot(turned[t], wide[slot_ref[t, rank]], preferred_element_type=F32)

    def links(k, rank):
        if k >= 2:
            mate_copy(k - 2, ranks[k - 2]).wait_send()

        def theirs(i, carry):
            t = (2 * (i // quarter) + 1 - core) * quarter + i % quarter
            msend[k % 2, i] = product(t, rank)
            return carry

        lax.fori_loop(0, 2 * quarter, theirs, 0, unroll=8)
        mate_copy(k, rank).start()

        def ours(i, carry):
            t = (2 * (i // quarter) + core) * quarter + i % quarter
            own[k % 2, i] = product(t, rank)
            return carry

        lax.fori_loop(0, 2 * quarter, ours, 0, unroll=8)

    def finish(k):
        rank = ranks[k]
        if k >= 2:
            across_copy(k - 2, ranks[k - 2]).wait_send()
        mate_copy(k, rank).wait_recv()

        def send(j, carry):
            i = (1 - half) * quarter + j
            ysend[k % 2, j] = own[k % 2, i] + mrecv[rank, i]
            return carry

        lax.fori_loop(0, quarter, send, 0)
        across_copy(k, rank).start()

        def hold(j, carry):
            i = half * quarter + j
            keep[rank, j] = own[k % 2, i] + mrecv[rank, i]
            return carry

        lax.fori_loop(0, quarter, hold, 0)

    def process(rank):
        k = len(ranks)
        ranks.append(rank)
        links(k, rank)
        if k >= 1:
            finish(k - 1)

    expand(c_ref, dom_ref)

    def turn(t, carry):
        turned[t] = wide[t].astype(F32).T.astype(BF16)
        return carry

    lax.fori_loop(0, pc, turn, 0, unroll=2)
    process(p)
    for step in range(1, steps + 1):
        for c in (2, 0, 1):
            for d in (0, 1):
                if c in parts_of(step, d):
                    arrive(step, d, c)
                if step < steps and c in parts_of(step + 1, d):
                    move(step + 1, d, c).start()
        for d in (0, 1) if step < steps else (0,):
            rank = at(position + (-step if d == 0 else step), n)
            expand(cbuf.at[rank], dbuf.at[rank])
            process(rank)
    finish(n - 1)
    for k in range(n):
        rank = ranks[k]
        across_copy(k, rank).wait_recv()

        def last(j, carry):
            out_ref[rank, j] = (keep[rank, j] + yrecv[rank, j]).astype(BF16)
            return carry

        lax.fori_loop(0, quarter, last, 0)
    for k in (n - 2, n - 1):
        mate_copy(k, ranks[k]).wait_send()
        across_copy(k, ranks[k]).wait_send()
    for step in range(1, steps + 1):
        for d in (0, 1):
            for c in parts_of(step, d):
                move(step, d, c).wait_send()


def iteration(
    n, first, slot_ref, fock_ref, shift_ref, start_ref, x_ref, k_ref, e_ref, out_ref,
    abuf, stage, acc, mine, theirs, rs, rr, ms, mr, ys, yr, fs, fr,
):
    p, g, position, mate, across = places(n)
    pc = k_ref.shape[0]
    width = k_ref.shape[1]
    quarter = pc // 4
    steps = n // 2
    right, left = at(position + 1, n), at(position - 1, n)
    peers = [(right, g), (left, g), (p, mate), (p, across)]
    diagonal = 3 - g
    if not first:
        peers.append((p, diagonal))
    greet(peers)
    parts_of = ring_parts(steps, 2)

    def span(rank, c):
        group = g if c == 0 else across
        return abuf.at[pl.ds(rank * pc + group * quarter, quarter)]

    def move(step, direction, c):
        offset = -(step - 1) if direction == 0 else step - 1
        ref = span(at(position + offset, n), c)
        src = start_ref if (step == 1 and c == 0 and not first) else ref
        return remote(
            src, ref, rs.at[direction, step - 1, c], rr.at[direction, step - 1, c],
            (right if direction == 0 else left, g),
        )

    def arrive(step, direction, c):
        offset = -step if direction == 0 else step
        ref = span(at(position + offset, n), c)
        remote(
            ref, ref, rs.at[direction, step - 1, c], rr.at[direction, step - 1, c],
            (left if direction == 0 else right, g),
        ).wait_recv()

    def mate_copy(k, rank, c, src=None):
        ref = span(rank, c)
        return remote(ref if src is None else src, ref, ms.at[k, c], mr.at[k, c], (p, mate))

    def mate_wait(k, rank, c):
        group = mate if c == 0 else 3 - g
        ref = abuf.at[pl.ds(rank * pc + group * quarter, quarter)]
        remote(ref, ref, ms.at[k, c], mr.at[k, c], (p, mate)).wait_recv()

    if first:
        def copy_own(i, carry):
            abuf[p * pc + i] = start_ref[i].astype(BF16)
            return carry

        for c in (0, 1):
            group = g if c == 0 else across
            lax.fori_loop(group * quarter, (group + 1) * quarter, copy_own, 0)
            for d in (0, 1):
                if c in parts_of(1, d):
                    move(1, d, c).start()
        for group in (mate, 3 - g):
            lax.fori_loop(group * quarter, (group + 1) * quarter, copy_own, 0)
    else:
        ycopy = remote(
            start_ref, span(p, 0), ys, yr, (p, across)
        )
        ycopy.start()
        for d in (0, 1):
            move(1, d, 0).start()
        mate_copy(0, p, 0, start_ref).start()

        def copy_own(i, carry):
            abuf[p * pc + g * quarter + i] = start_ref[i]
            return carry

        lax.fori_loop(0, quarter, copy_own, 0)
        ref = span(p, 1)
        remote(ref, ref, ys, yr, (p, across)).wait_recv()
        for d in (0, 1):
            move(1, d, 1).start()
        mate_copy(0, p, 1).start()
        mate_wait(0, p, 0)
        mate_wait(0, p, 1)

    acc[...] = jnp.zeros_like(acc)

    def couple(rank):
        def copy(i, carry):
            stage[i] = abuf[rank * pc + i]
            return carry

        lax.fori_loop(0, pc, copy, 0, unroll=4)

        def one(j, carry):
            t = g * quarter + j
            source = stage[slot_ref[t, rank]]
            x = x_ref[rank, j]
            h = jnp.dot(x, source, preferred_element_type=F32).astype(BF16)
            y = lax.dot_general(h, x, (((1,), (1,)), ((), ())), preferred_element_type=F32)
            acc[j] += fock_ref[t, rank] * y
            return carry

        lax.fori_loop(0, quarter, one, 0, unroll=4)

    couple(p)
    pending = []
    k = 0
    for step in range(1, steps + 1):
        for c in (0, 1):
            for d in (0, 1):
                rank = at(position + (-step if d == 0 else step), n)
                if c in parts_of(step, d):
                    arrive(step, d, c)
                    if step < steps and c in parts_of(step + 1, d):
                        move(step + 1, d, c).start()
                    kk = 2 * step - 1 + (d if step < steps else 0)
                    mate_copy(kk, rank, c).start()
        for kk, rank in pending:
            for c in (0, 1):
                mate_wait(kk, rank, c)
            couple(rank)
        pending = []
        for d in (0, 1) if step < steps else (0,):
            pending.append((2 * step - 1 + d, at(position + (-step if d == 0 else step), n)))
    for kk, rank in pending:
        for c in (0, 1):
            mate_wait(kk, rank, c)
        couple(rank)

    def scaled(t, total):
        row = jnp.broadcast_to(e_ref[pl.ds(t, 1), :], (width, width))
        return -(k_ref[t] + total) / (row.T + row + shift_ref[t, 0])

    if first:
        def result(j, carry):
            out_ref[j] = scaled(g * quarter + j, acc[j]).astype(BF16)
            return carry

        lax.fori_loop(0, quarter, result, 0)
    else:
        def pack(j, carry):
            mine[j] = acc[j]
            return carry

        lax.fori_loop(0, quarter, pack, 0)
        others = (across, diagonal, mate)
        for i, other in enumerate(others):
            remote(mine, theirs.at[i], fs.at[i], fr.at[i], (p, other)).start()

        def result(j, carry):
            t = g * quarter + j
            out_ref[t] = scaled(t, acc[j])
            return carry

        lax.fori_loop(0, quarter, result, 0)
        for i in (2, 0, 1):
            other = others[i]
            copy = remote(mine, theirs.at[i], fs.at[i], fr.at[i], (p, other))
            copy.wait_recv()

            def rest(j, carry):
                t = other * quarter + j
                out_ref[t] = scaled(t, theirs[i, j])
                return carry

            lax.fori_loop(0, quarter, rest, 0)
        for i, other in enumerate(others):
            remote(mine, theirs.at[i], fs.at[i], fr.at[i], (p, other)).wait_send()
        remote(start_ref, span(p, 0), ys, yr, (p, across)).wait_send()
        mate_copy(0, p, 0, start_ref).wait_send()
        mate_copy(0, p, 1).wait_send()
    for kk in range(1, n):
        for c in (0, 1):
            mate_copy(kk, p, c).wait_send()
    for step in range(1, steps + 1):
        for d in (0, 1):
            for c in parts_of(step, d):
                move(step, d, c).wait_send()


def on_device(
    coefficients, domain, coupling_owner, coupling_slot, coupling_fock,
    exchange_integrals, pno_energy, pair_shift, amplitudes_start,
):
    n = lax.axis_size("pairs")
    pc, rows, width = coefficients.shape
    quarter = pc // lax.axis_size("grp")
    steps = n // 2
    named = coupling_owner[:, :, None] == jnp.arange(n, dtype=jnp.int32)[None, None, :]
    slots = jnp.sum(jnp.where(named, coupling_slot[:, :, None], 0), axis=1)
    focks = jnp.sum(jnp.where(named, coupling_fock[:, :, None], 0.0), axis=1)
    vmem, smem = pl.BlockSpec(memory_space=pltpu.VMEM), pl.BlockSpec(memory_space=pltpu.SMEM)
    dma = pltpu.SemaphoreType.DMA

    def params(collective):
        return pltpu.CompilerParams(
            collective_id=collective, has_side_effects=True, vmem_limit_bytes=60 * 2**20
        )

    x = pl.pallas_call(
        functools.partial(intersections, n),
        out_shape=jax.ShapeDtypeStruct((n, quarter, width, width), BF16),
        in_specs=[smem, vmem, vmem],
        out_specs=vmem,
        scratch_shapes=[
            pltpu.VMEM((n, pc, rows, width), BF16),
            pltpu.VMEM((n, pc, rows), jnp.int32),
            pltpu.VMEM((pc, width, NB), BF16),
            pltpu.VMEM((pc, NB, width), BF16),
            pltpu.VMEM((2, 2 * quarter, width, width), F32),
            pltpu.VMEM((2, 2 * quarter, width, width), F32),
            pltpu.VMEM((n, 2 * quarter, width, width), F32),
            pltpu.VMEM((2, quarter, width, width), F32),
            pltpu.VMEM((n, quarter, width, width), F32),
            pltpu.VMEM((n, quarter, width, width), F32),
            dma((2, steps, 3)), dma((2, steps, 3)),
            dma((n,)), dma((n,)), dma((n,)), dma((n,)),
        ],
        compiler_params=params(0),
        name="intersections",
    )(slots, coefficients, domain)

    def iterate(first, start):
        shape = (quarter, width, width) if first else (pc, width, width)
        return pl.pallas_call(
            functools.partial(iteration, n, first),
            out_shape=jax.ShapeDtypeStruct(shape, BF16 if first else F32),
            in_specs=[smem, smem, smem, vmem, vmem, vmem, vmem],
            out_specs=vmem,
            scratch_shapes=[
                pltpu.VMEM((n * pc, width, width), BF16),
                pltpu.VMEM((pc, width, width), BF16),
                pltpu.VMEM((quarter, width, width), F32),
                pltpu.VMEM((quarter, width, width), F32),
                pltpu.VMEM((3, quarter, width, width), F32),
                dma((2, steps, 2)), dma((2, steps, 2)),
                dma((n, 2)), dma((n, 2)), dma, dma, dma((3,)), dma((3,)),
            ],
            compiler_params=params(1 if first else 2),
            name="first" if first else "second",
        )(slots, focks, pair_shift.reshape(-1, 1), start, x, exchange_integrals, pno_energy)

    return iterate(False, iterate(True, amplitudes_start))


def solution(mesh):
    placed = (
        P("pairs", "grp", None),
        P("pairs", "grp"),
        P("pairs", None),
        P("pairs", None),
        P("pairs", None),
        P("pairs", None, None),
        P("pairs", None),
        P("pairs"),
        P("pairs", None, None),
    )
    return jax.shard_map(
        on_device, mesh=mesh, in_specs=placed, out_specs=P("pairs", None, None), check_vma=False
    )
```

time: 525 us -> 147 us (0.28)
  blocking collectives: 342 us -> 0 us
  Pallas kernels: 0 us -> 142 us
  waiting for transfers between devices: 90.2 us -> 0 us
  other arithmetic: 25.8 us -> 0.73 us
  local copies, waits for them, and re-layouts: 28.6 us -> 4.33 us
  matrix products: 21.5 us -> 0 us
  starting transfers between devices: 15.3 us -> 0 us
    all_to_all x2 -> x0, blocking collectives: 196 us -> none  [the longest x1 98.6 us: on_device(): lax.all_to_all(outgoing_amp, 'pairs', split_axis=0, concat_axis=0, tiled=...]
    psum x1 -> x0, blocking collectives: 146 us -> none  [on_device(): lax.psum(jnp.einsum('pra,kprc->kpac', coefficients, gathered, preferred_e...]
    pallas_call x0 -> x3, Pallas kernels: none -> 142 us  [the longest x2 74.7 us: iterate(): pl.pallas_call(functools.partial(iteration, n, first), out_shape=jax.Shap...]
    all_to_all x3 -> x0, waiting for transfers between devices: 90.2 us -> none  [the longest x1 85.8 us: on_device(): lax.all_to_all(outgoing_amp, 'pairs', split_axis=0, concat_axis=0, tiled=...]
    gather x8 -> x0, local copies, waits for them, and re-layouts: 26.1 us -> none  [the longest x2 10.5 us: on_device(): jnp.take(incoming_amp.reshape(pair_ranks * capacity, pno_count, pno_count...]
    dot_general x3 -> x0, matrix products: 21.5 us -> none  [the longest x2 15 us: on_device(): jnp.einsum('kpad,kpbd->kpab', half_proj, intersection_half, preferred_ele...]
    select_n x9 -> x0, other arithmetic: 20 us -> none  [the longest x2 10.6 us: on_device(): jnp.take(incoming_amp.reshape(pair_ranks * capacity, pno_count, pno_count...]
    all_to_all x3 -> x0, starting transfers between devices: 15.3 us -> none  [the longest x1 7.28 us: on_device(): lax.all_to_all(request, 'pairs', split_axis=0, concat_axis=0, tiled=True)]
  transfers between devices with their start and end apart: 3 -> 0, of which waited for: 2 -> 0; matrix products, arithmetic and copies ran while one was open for 4% -> 0% of each run, Pallas kernels for 0% -> 0%
where the time goes in v1:
time: 147 us
  Pallas kernels  142 us (97%)
  local copies, waits for them, and re-layouts  4.33 us (3%)
    pallas_call x2, Pallas kernels, iterate(): pl.pallas_call(functools.partial(iteration, n, first), out_shape=jax.Shap...  74.7 us
    pallas_call x1, Pallas kernels, on_device(): pl.pallas_call(functools.partial(intersections, n), out_shape=jax.ShapeDt...  67.1 us

profile of v1, /device:TPU:0, one launch (start us, length us, event | category | flops | bytes accessed | tf_op | source)
XLA Modules:
  0.0 146.9 jit_solution(12036536068575866423)
XLA Ops:
  0.0 0.7 select_reduce_fusion.1
  0.7 0.0 copy-start
  0.7 0.0 copy-start.1
  0.7 0.7 copy.19.slot_ref
  1.4 0.0 copy-done
  1.4 0.0 copy-done.1
  1.4 0.0 copy-start.2
  1.4 0.7 copy.20.fock_ref
  2.1 0.0 copy-done.2
  2.1 0.7 copy.21.shift_ref
  2.8 67.1 %intersections.1.x_ref = bf16[8,4,128,128]{3,2,1,0:T(8,128)(2,1)} custom-call(s32[16,8]{1,0:T(8,128)} %copy.19.slot_ref, bf16[16,128,128]{2,1,0:T(8,128)(2,1)} %c_ref.1, s32[16,128]{1,0:T(8,128)} %dom_ref.1), custom_call_target="tpu_custom_call" | custom-call | tf_op jit(solution)/shard_map/intersections/pallas_call | solution.py:414
  69.9 29.8 %first.1.start_ref = bf16[4,128,128]{2,1,0:T(8,128)(2,1)} custom-call(s32[16,8]{1,0:T(8,128)} %copy.19.slot_ref, f32[16,8]{1,0:T(8,128)} %copy.20.fock_ref, f32[16,1]{1,0:T(8,128)} %copy.21.shift_ref, f32[16,128,128]{2,1,0:T(8,128)} %start_ref.1, bf16[8,4,128,128]{3,2,1,0:T(8,128)(2,1)} %intersections.1.x_ref, f32[16,128,128]{2,1,0:T(8,128)} %k_ref.3, ...), custom_call_target="tpu_custom_call" | custom-call | tf_op jit(solution)/shard_map/first/pallas_call | solution.py:439
  99.7 45.0 %second.1 = f32[16,128,128]{2,1,0:T(8,128)} custom-call(s32[16,8]{1,0:T(8,128)} %copy.19.slot_ref, f32[16,8]{1,0:T(8,128)} %copy.20.fock_ref, f32[16,1]{1,0:T(8,128)} %copy.21.shift_ref, bf16[4,128,128]{2,1,0:T(8,128)(2,1)} %first.1.start_ref, bf16[8,4,128,128]{3,2,1,0:T(8,128)(2,1)} %intersections.1.x_ref, f32[16,128,128]{2,1,0:T(8,128)} %k_ref.3, ...), custom_call_target="tpu_custom_call" | custom-call | tf_op jit(solution)/shard_map/second/pallas_call | solution.py:439
  144.6 2.3 %copy.23 = f32[16,128,128]{2,1,0:T(8,128)} copy(f32[16,128,128]{2,1,0:T(8,128)} %second.1) | data formatting | bytes 2097152
  (1 shorter events, 0.0 us)
Async XLA Ops:
  0.7 0.7 copy-start
  0.7 0.7 copy-start.1
  1.4 0.7 copy-start.2

commit v2 on v1

--- a/solution.py
+++ b/solution.py
@@ -173,8 +173,6 @@
         k = len(ranks)
         ranks.append(rank)
         links(k, rank)
-        if k >= 1:
-            finish(k - 1)
 
     expand(c_ref, dom_ref)
 
@@ -184,6 +182,7 @@
 
     lax.fori_loop(0, pc, turn, 0, unroll=2)
     process(p)
+    finish(0)
     for step in range(1, steps + 1):
         for c in (2, 0, 1):
             for d in (0, 1):
@@ -195,7 +194,9 @@
             rank = at(position + (-step if d == 0 else step), n)
             expand(cbuf.at[rank], dbuf.at[rank])
             process(rank)
-    finish(n - 1)
+            if d == 1:
+                finish(len(ranks) - 2)
+        finish(len(ranks) - 1)
     for k in range(n):
         rank = ranks[k]
         across_copy(k, rank).wait_recv()
@@ -215,30 +216,32 @@
 
 
 def iteration(
-    n, first, slot_ref, fock_ref, shift_ref, start_ref, x_ref, k_ref, e_ref, out_ref,
-    abuf, stage, acc, mine, theirs, rs, rr, ms, mr, ys, yr, fs, fr,
+    n, first, slot_ref, fock_ref, start_ref, x_ref, k_ref, e_ref, out_ref,
+    abuf, stage, acc, mine, rs, rr, ms, mr, ys, yr, fs, fr,
 ):
     p, g, position, mate, across = places(n)
     pc = k_ref.shape[0]
     width = k_ref.shape[1]
     quarter = pc // 4
+    eighth = quarter // 2
     steps = n // 2
     right, left = at(position + 1, n), at(position - 1, n)
-    peers = [(right, g), (left, g), (p, mate), (p, across)]
     diagonal = 3 - g
-    if not first:
-        peers.append((p, diagonal))
-    greet(peers)
-    parts_of = ring_parts(steps, 2)
+    greet([(right, g), (left, g), (p, mate), (p, across)])
+    parts_of = ring_parts(steps, 3)
+
+    def chunk(rank, group, c):
+        return abuf.at[pl.ds(rank * pc + group * quarter + (c % 2) * eighth, eighth)]
 
     def span(rank, c):
-        group = g if c == 0 else across
-        return abuf.at[pl.ds(rank * pc + group * quarter, quarter)]
-
-    def move(step, direction, c):
+        return chunk(rank, g if c < 2 else across, c)
+
+    def ring_copy(step, direction, c):
         offset = -(step - 1) if direction == 0 else step - 1
         ref = span(at(position + offset, n), c)
-        src = start_ref if (step == 1 and c == 0 and not first) else ref
+        src = ref
+        if step == 1 and c < 2 and not first:
+            src = start_ref.at[pl.ds(c * eighth, eighth)]
         return remote(
             src, ref, rs.at[direction, step - 1, c], rr.at[direction, step - 1, c],
             (right if direction == 0 else left, g),
@@ -256,45 +259,65 @@
         ref = span(rank, c)
         return remote(ref if src is None else src, ref, ms.at[k, c], mr.at[k, c], (p, mate))
 
-    def mate_wait(k, rank, c):
-        group = mate if c == 0 else 3 - g
-        ref = abuf.at[pl.ds(rank * pc + group * quarter, quarter)]
-        remote(ref, ref, ms.at[k, c], mr.at[k, c], (p, mate)).wait_recv()
+    def mate_wait(k, rank):
+        for c in range(4):
+            ref = chunk(rank, mate if c < 2 else diagonal, c)
+            remote(ref, ref, ms.at[k, c], mr.at[k, c], (p, mate)).wait_recv()
+
+    def across_copy(k, rank, c=1, src=None):
+        ref = span(rank, c)
+        sem = k if c == 1 else n
+        return remote(ref if src is None else src, ref, ys.at[sem], yr.at[sem], (p, across))
+
+    def across_wait(k, rank, c=3):
+        ref = span(rank, c)
+        sem = k if c == 3 else n
+        remote(ref, ref, ys.at[sem], yr.at[sem], (p, across)).wait_recv()
+
+    def own_half(c):
+        return start_ref.at[pl.ds(c * eighth, eighth)]
 
     if first:
         def copy_own(i, carry):
             abuf[p * pc + i] = start_ref[i].astype(BF16)
             return carry
 
+        def group_in(group):
+            lax.fori_loop(group * quarter, (group + 1) * quarter, copy_own, 0)
+
+        group_in(g)
         for c in (0, 1):
-            group = g if c == 0 else across
-            lax.fori_loop(group * quarter, (group + 1) * quarter, copy_own, 0)
             for d in (0, 1):
                 if c in parts_of(1, d):
-                    move(1, d, c).start()
-        for group in (mate, 3 - g):
-            lax.fori_loop(group * quarter, (group + 1) * quarter, copy_own, 0)
+                    ring_copy(1, d, c).start()
+        group_in(across)
+        for d in (0, 1):
+            if 2 in parts_of(1, d):
+                ring_copy(1, d, 2).start()
+        group_in(mate)
+        group_in(diagonal)
     else:
-        ycopy = remote(
-            start_ref, span(p, 0), ys, yr, (p, across)
-        )
-        ycopy.start()
-        for d in (0, 1):
-            move(1, d, 0).start()
-        mate_copy(0, p, 0, start_ref).start()
+        for c in (0, 1):
+            across_copy(0, p, c, own_half(c)).start()
+            for d in (0, 1):
+                if c in parts_of(1, d):
+                    ring_copy(1, d, c).start()
+        for c in (0, 1):
+            mate_copy(0, p, c, own_half(c)).start()
 
         def copy_own(i, carry):
             abuf[p * pc + g * quarter + i] = start_ref[i]
             return carry
 
         lax.fori_loop(0, quarter, copy_own, 0)
-        ref = span(p, 1)
-        remote(ref, ref, ys, yr, (p, across)).wait_recv()
+        across_wait(0, p, 2)
         for d in (0, 1):
-            move(1, d, 1).start()
-        mate_copy(0, p, 1).start()
-        mate_wait(0, p, 0)
-        mate_wait(0, p, 1)
+            if 2 in parts_of(1, d):
+                ring_copy(1, d, 2).start()
+        mate_copy(0, p, 2).start()
+        across_wait(0, p, 3)
+        mate_copy(0, p, 3).start()
+        mate_wait(0, p)
 
     acc[...] = jnp.zeros_like(acc)
 
@@ -317,79 +340,89 @@
         lax.fori_loop(0, quarter, one, 0, unroll=4)
 
     couple(p)
-    pending = []
-    k = 0
+
+    def exchange(blocks):
+        for k, rank in blocks:
+            across_wait(k, rank)
+            mate_copy(k, rank, 3).start()
+
+    def use(blocks):
+        for k, rank in blocks:
+            mate_wait(k, rank)
+            couple(rank)
+
+    landed, shared = [], []
     for step in range(1, steps + 1):
-        for c in (0, 1):
+        for c in (1, 0, 2):
             for d in (0, 1):
                 rank = at(position + (-step if d == 0 else step), n)
                 if c in parts_of(step, d):
                     arrive(step, d, c)
                     if step < steps and c in parts_of(step + 1, d):
-                        move(step + 1, d, c).start()
-                    kk = 2 * step - 1 + (d if step < steps else 0)
-                    mate_copy(kk, rank, c).start()
-        for kk, rank in pending:
-            for c in (0, 1):
-                mate_wait(kk, rank, c)
-            couple(rank)
-        pending = []
-        for d in (0, 1) if step < steps else (0,):
-            pending.append((2 * step - 1 + d, at(position + (-step if d == 0 else step), n)))
-    for kk, rank in pending:
-        for c in (0, 1):
-            mate_wait(kk, rank, c)
-        couple(rank)
-
-    def scaled(t, total):
+                        ring_copy(step + 1, d, c).start()
+                    k = 2 * step - 1 + (d if step < steps else 0)
+                    if c == 1:
+                        across_copy(k, rank).start()
+                    mate_copy(k, rank, c).start()
+        exchange(landed)
+        use(shared)
+        shared = landed
+        landed = [
+            (2 * step - 1 + d, at(position + (-step if d == 0 else step), n))
+            for d in ((0, 1) if step < steps else (0,))
+        ]
+    exchange(landed)
+    use(shared)
+    use(landed)
+
+    def scaled(j):
+        t = g * quarter + j
         row = jnp.broadcast_to(e_ref[pl.ds(t, 1), :], (width, width))
-        return -(k_ref[t] + total) / (row.T + row + shift_ref[t, 0])
+        return (-(k_ref[t] + acc[j]) / (row.T + row + fock_ref[t, n])).astype(BF16)
 
     if first:
         def result(j, carry):
-            out_ref[j] = scaled(g * quarter + j, acc[j]).astype(BF16)
-            return carry
-
-        lax.fori_loop(0, quarter, result, 0)
+            out_ref[j] = scaled(j)
+            return carry
+
+        lax.fori_loop(0, quarter, result, 0, unroll=2)
     else:
-        def pack(j, carry):
-            mine[j] = acc[j]
-            return carry
-
-        lax.fori_loop(0, quarter, pack, 0)
-        others = (across, diagonal, mate)
-        for i, other in enumerate(others):
-            remote(mine, theirs.at[i], fs.at[i], fr.at[i], (p, other)).start()
+        def block(ref, group):
+            return ref.at[pl.ds(group * quarter, quarter)]
 
         def result(j, carry):
-            t = g * quarter + j
-            out_ref[t] = scaled(t, acc[j])
-            return carry
-
-        lax.fori_loop(0, quarter, result, 0)
-        for i in (2, 0, 1):
-            other = others[i]
-            copy = remote(mine, theirs.at[i], fs.at[i], fr.at[i], (p, other))
-            copy.wait_recv()
-
-            def rest(j, carry):
-                t = other * quarter + j
-                out_ref[t] = scaled(t, theirs[i, j])
-                return carry
-
-            lax.fori_loop(0, quarter, rest, 0)
-        for i, other in enumerate(others):
-            remote(mine, theirs.at[i], fs.at[i], fr.at[i], (p, other)).wait_send()
-        remote(start_ref, span(p, 0), ys, yr, (p, across)).wait_send()
-        mate_copy(0, p, 0, start_ref).wait_send()
-        mate_copy(0, p, 1).wait_send()
-    for kk in range(1, n):
-        for c in (0, 1):
-            mate_copy(kk, p, c).wait_send()
+            value = scaled(j)
+            mine[j] = value
+            out_ref[g * quarter + j] = value
+            return carry
+
+        lax.fori_loop(0, quarter, result, 0, unroll=2)
+        over = remote(mine, block(out_ref, g), fs.at[0], fr.at[0], (p, across))
+        beside = remote(mine, block(out_ref, g), fs.at[1], fr.at[1], (p, mate))
+        corner = remote(
+            block(out_ref, across), block(out_ref, across), fs.at[2], fr.at[2], (p, mate)
+        )
+        over.start()
+        beside.start()
+        remote(mine, block(out_ref, across), fs.at[0], fr.at[0], (p, across)).wait_recv()
+        corner.start()
+        remote(mine, block(out_ref, mate), fs.at[1], fr.at[1], (p, mate)).wait_recv()
+        remote(mine, block(out_ref, diagonal), fs.at[2], fr.at[2], (p, mate)).wait_recv()
+        over.wait_send()
+        beside.wait_send()
+        corner.wait_send()
+        across_copy(0, p, 0, own_half(0)).wait_send()
+        across_copy(0, p, 1, own_half(1)).wait_send()
+        for c in range(4):
+            mate_copy(0, p, c).wait_send()
+    for k in range(1, n):
+        across_copy(k, p).wait_send()
+        for c in range(4):
+            mate_copy(k, p, c).wait_send()
     for step in range(1, steps + 1):
         for d in (0, 1):
             for c in parts_of(step, d):
-                move(step, d, c).wait_send()
+                ring_copy(step, d, c).wait_send()
 
 
 def on_device(
@@ -403,6 +436,7 @@
     named = coupling_owner[:, :, None] == jnp.arange(n, dtype=jnp.int32)[None, None, :]
     slots = jnp.sum(jnp.where(named, coupling_slot[:, :, None], 0), axis=1)
     focks = jnp.sum(jnp.where(named, coupling_fock[:, :, None], 0.0), axis=1)
+    focks = jnp.concatenate([focks, pair_shift[:, None]], axis=1)
     vmem, smem = pl.BlockSpec(memory_space=pltpu.VMEM), pl.BlockSpec(memory_space=pltpu.SMEM)
     dma = pltpu.SemaphoreType.DMA
 
@@ -438,23 +472,22 @@
         shape = (quarter, width, width) if first else (pc, width, width)
         return pl.pallas_call(
             functools.partial(iteration, n, first),
-            out_shape=jax.ShapeDtypeStruct(shape, BF16 if first else F32),
-            in_specs=[smem, smem, smem, vmem, vmem, vmem, vmem],
+            out_shape=jax.ShapeDtypeStruct(shape, BF16),
+            in_specs=[smem, smem, vmem, vmem, vmem, vmem],
             out_specs=vmem,
             scratch_shapes=[
                 pltpu.VMEM((n * pc, width, width), BF16),
                 pltpu.VMEM((pc, width, width), BF16),
                 pltpu.VMEM((quarter, width, width), F32),
-                pltpu.VMEM((quarter, width, width), F32),
-                pltpu.VMEM((3, quarter, width, width), F32),
-                dma((2, steps, 2)), dma((2, steps, 2)),
-                dma((n, 2)), dma((n, 2)), dma, dma, dma((3,)), dma((3,)),
+                pltpu.VMEM((quarter, width, width), BF16),
+                dma((2, steps, 3)), dma((2, steps, 3)),
+                dma((n, 4)), dma((n, 4)), dma((n + 1,)), dma((n + 1,)), dma((3,)), dma((3,)),
             ],
             compiler_params=params(1 if first else 2),
             name="first" if first else "second",
-        )(slots, focks, pair_shift.reshape(-1, 1), start, x, exchange_integrals, pno_energy)
-
-    return iterate(False, iterate(True, amplitudes_start))
+        )(slots, focks, start, x, exchange_integrals, pno_energy)
+
+    return iterate(False, iterate(True, amplitudes_start)).astype(F32)
 
 
 def solution(mesh):

time: 147 us -> 132 us (0.90)
  Pallas kernels: 142 us -> 126 us
  local copies, waits for them, and re-layouts: 4.33 us -> 1.42 us
  other arithmetic: 0.73 us -> 3.52 us
    pallas_call x2, Pallas kernels: 74.7 us -> 61.1 us  [iterate(): pl.pallas_call(functools.partial(iteration, n, first), out_shape=jax.Shap...]
    convert_element_type x0 -> x1, other arithmetic: none -> 2.12 us  [on_device(): return iterate(False, iterate(True, amplitudes_start)).astype(F32)]
    pallas_call x1, Pallas kernels: 67.1 us -> 65.2 us  [on_device(): pl.pallas_call(functools.partial(intersections, n), out_shape=jax.ShapeDt...]
    unnamed x7 -> x6, local copies, waits for them, and re-layouts: 2.32 us -> 0.6 us
where the time goes in v2:
time: 132 us; the launch traced here: 131 us
  Pallas kernels  126 us (95%)
  other arithmetic  3.52 us (3%)
  local copies, waits for them, and re-layouts  1.42 us (1%)
    pallas_call x1, Pallas kernels, on_device(): pl.pallas_call(functools.partial(intersections, n), out_shape=jax.ShapeDt...  65.2 us
    pallas_call x2, Pallas kernels, iterate(): pl.pallas_call(functools.partial(iteration, n, first), out_shape=jax.Shap...  61.1 us

profile of v2, /device:TPU:0, one launch (start us, length us, event | category | flops | bytes accessed | tf_op | source)
XLA Modules:
  0.0 131.2 jit_solution(9044238044125125584)
XLA Ops:
  0.0 0.7 select_reduce_fusion.1
  0.7 0.0 copy-start
  0.7 0.0 copy-start.1
  0.7 0.7 copy.18.slot_ref
  1.4 0.0 copy-done
  1.4 0.0 copy-done.1
  1.4 0.0 copy-start.2
  1.4 0.1 copy.14
  1.5 0.6 copy-done.2
  2.1 0.1 copy.15
  2.2 0.7 pad_maximum_fusion.fock_ref
  2.9 65.2 %intersections.1.x_ref = bf16[8,4,128,128]{3,2,1,0:T(8,128)(2,1)} custom-call(s32[16,8]{1,0:T(8,128)} %copy.18.slot_ref, bf16[16,128,128]{2,1,0:T(8,128)(2,1)} %c_ref.1, s32[16,128]{1,0:T(8,128)} %dom_ref.1), custom_call_target="tpu_custom_call" | custom-call | tf_op jit(solution)/shard_map/intersections/pallas_call | solution.py:448
  68.0 27.3 %first.1.start_ref = bf16[4,128,128]{2,1,0:T(8,128)(2,1)} custom-call(s32[16,8]{1,0:T(8,128)} %copy.18.slot_ref, f32[16,9]{1,0:T(8,128)} %pad_maximum_fusion.fock_ref, f32[16,128,128]{2,1,0:T(8,128)} %start_ref.1, bf16[8,4,128,128]{3,2,1,0:T(8,128)(2,1)} %intersections.1.x_ref, f32[16,128,128]{2,1,0:T(8,128)} %k_ref.3, f32[16,128]{1,0:T(8,128)} %e_ref.3), custom_call_target="tpu_custom_call" | custom-call | tf_op jit(solution)/shard_map/first/pallas_call | solution.py:473
  95.4 33.7 %second.1 = bf16[16,128,128]{2,1,0:T(8,128)(2,1)} custom-call(s32[16,8]{1,0:T(8,128)} %copy.18.slot_ref, f32[16,9]{1,0:T(8,128)} %pad_maximum_fusion.fock_ref, bf16[4,128,128]{2,1,0:T(8,128)(2,1)} %first.1.start_ref, bf16[8,4,128,128]{3,2,1,0:T(8,128)(2,1)} %intersections.1.x_ref, f32[16,128,128]{2,1,0:T(8,128)} %k_ref.3, f32[16,128]{1,0:T(8,128)} %e_ref.3), custom_call_target="tpu_custom_call" | custom-call | tf_op jit(solution)/shard_map/second/pallas_call | solution.py:473
  129.1 2.1 %convert_element_type.3 = f32[16,128,128]{2,1,0:T(8,128)} convert(bf16[16,128,128]{2,1,0:T(8,128)(2,1)} %second.1) | non-fusion elementwise | flops 262144 | bytes 1572864 | tf_op jit(solution)/shard_map/convert_element_type | solution.py:490
  (1 shorter events, 0.0 us)
Async XLA Ops:
  0.7 0.7 copy-start
  0.7 0.7 copy-start.1
  1.4 0.7 copy-start.2

commit v3 on v2

--- a/solution.py
+++ b/solution.py
@@ -190,6 +190,8 @@
                     arrive(step, d, c)
                 if step < steps and c in parts_of(step + 1, d):
                     move(step + 1, d, c).start()
+        if step == steps - 1:
+            yield None
         for d in (0, 1) if step < steps else (0,):
             rank = at(position + (-step if d == 0 else step), n)
             expand(cbuf.at[rank], dbuf.at[rank])
@@ -197,7 +199,7 @@
             if d == 1:
                 finish(len(ranks) - 2)
         finish(len(ranks) - 1)
-    for k in range(n):
+    def settle(k):
         rank = ranks[k]
         across_copy(k, rank).wait_recv()
 
@@ -206,6 +208,8 @@
             return carry
 
         lax.fori_loop(0, quarter, last, 0)
+
+    yield settle
     for k in (n - 2, n - 1):
         mate_copy(k, ranks[k]).wait_send()
         across_copy(k, ranks[k]).wait_send()
@@ -216,7 +220,7 @@
 
 
 def iteration(
-    n, first, slot_ref, fock_ref, start_ref, x_ref, k_ref, e_ref, out_ref,
+    n, first, joined, slot_ref, fock_ref, start_ref, x_ref, k_ref, e_ref, out_ref,
     abuf, stage, acc, mine, rs, rr, ms, mr, ys, yr, fs, fr,
 ):
     p, g, position, mate, across = places(n)
@@ -227,8 +231,10 @@
     steps = n // 2
     right, left = at(position + 1, n), at(position - 1, n)
     diagonal = 3 - g
-    greet([(right, g), (left, g), (p, mate), (p, across)])
-    parts_of = ring_parts(steps, 3)
+    if not joined:
+        greet([(right, g), (left, g), (p, mate), (p, across)])
+    parts = 4 if joined else 3
+    parts_of = ring_parts(steps, parts)
 
     def chunk(rank, group, c):
         return abuf.at[pl.ds(rank * pc + group * quarter + (c % 2) * eighth, eighth)]
@@ -291,9 +297,10 @@
                 if c in parts_of(1, d):
                     ring_copy(1, d, c).start()
         group_in(across)
-        for d in (0, 1):
-            if 2 in parts_of(1, d):
-                ring_copy(1, d, 2).start()
+        for c in range(2, parts):
+            for d in (0, 1):
+                if c in parts_of(1, d):
+                    ring_copy(1, d, c).start()
         group_in(mate)
         group_in(diagonal)
     else:
@@ -319,9 +326,13 @@
         mate_copy(0, p, 3).start()
         mate_wait(0, p)
 
+    settle = yield None
     acc[...] = jnp.zeros_like(acc)
 
-    def couple(rank):
+    def couple(rank, k):
+        if settle is not None:
+            settle(k)
+
         def copy(i, carry):
             stage[i] = abuf[rank * pc + i]
             return carry
@@ -339,21 +350,21 @@
 
         lax.fori_loop(0, quarter, one, 0, unroll=4)
 
-    couple(p)
+    couple(p, 0)
 
     def exchange(blocks):
-        for k, rank in blocks:
+        for k, rank in () if joined else blocks:
             across_wait(k, rank)
             mate_copy(k, rank, 3).start()
 
     def use(blocks):
         for k, rank in blocks:
             mate_wait(k, rank)
-            couple(rank)
+            couple(rank, k)
 
     landed, shared = [], []
     for step in range(1, steps + 1):
-        for c in (1, 0, 2):
+        for c in (1, 0, 2, 3)[:parts]:
             for d in (0, 1):
                 rank = at(position + (-step if d == 0 else step), n)
                 if c in parts_of(step, d):
@@ -361,7 +372,7 @@
                     if step < steps and c in parts_of(step + 1, d):
                         ring_copy(step + 1, d, c).start()
                     k = 2 * step - 1 + (d if step < steps else 0)
-                    if c == 1:
+                    if c == 1 and not joined:
                         across_copy(k, rank).start()
                     mate_copy(k, rank, c).start()
         exchange(landed)
@@ -416,13 +427,49 @@
         for c in range(4):
             mate_copy(0, p, c).wait_send()
     for k in range(1, n):
-        across_copy(k, p).wait_send()
+        if not joined:
+            across_copy(k, p).wait_send()
         for c in range(4):
             mate_copy(k, p, c).wait_send()
     for step in range(1, steps + 1):
         for d in (0, 1):
             for c in parts_of(step, d):
                 ring_copy(step, d, c).wait_send()
+
+
+def intersections_alone(*args):
+    steps = intersections(*args)
+    next(steps)
+    settle = next(steps)
+    for k in range(args[0]):
+        settle(k)
+    next(steps, None)
+
+
+def iteration_alone(n, first, *args):
+    steps = iteration(n, first, False, *args)
+    next(steps)
+    try:
+        steps.send(None)
+    except StopIteration:
+        pass
+
+
+def opening(
+    n, made, slot_ref, fock_ref, c_ref, dom_ref, start_ref, k_ref, e_ref, x_ref, out_ref, *scratch
+):
+    blocks = intersections(n, slot_ref, c_ref, dom_ref, x_ref, *scratch[:made])
+    next(blocks)
+    amps = iteration(
+        n, True, True, slot_ref, fock_ref, start_ref, x_ref, k_ref, e_ref, out_ref, *scratch[made:]
+    )
+    next(amps)
+    settle = next(blocks)
+    try:
+        amps.send(settle)
+    except StopIteration:
+        pass
+    next(blocks, None)
 
 
 def on_device(
@@ -445,49 +492,66 @@
             collective_id=collective, has_side_effects=True, vmem_limit_bytes=60 * 2**20
         )
 
-    x = pl.pallas_call(
-        functools.partial(intersections, n),
-        out_shape=jax.ShapeDtypeStruct((n, quarter, width, width), BF16),
-        in_specs=[smem, vmem, vmem],
-        out_specs=vmem,
-        scratch_shapes=[
-            pltpu.VMEM((n, pc, rows, width), BF16),
-            pltpu.VMEM((n, pc, rows), jnp.int32),
-            pltpu.VMEM((pc, width, NB), BF16),
-            pltpu.VMEM((pc, NB, width), BF16),
-            pltpu.VMEM((2, 2 * quarter, width, width), F32),
-            pltpu.VMEM((2, 2 * quarter, width, width), F32),
-            pltpu.VMEM((n, 2 * quarter, width, width), F32),
-            pltpu.VMEM((2, quarter, width, width), F32),
-            pltpu.VMEM((n, quarter, width, width), F32),
-            pltpu.VMEM((n, quarter, width, width), F32),
-            dma((2, steps, 3)), dma((2, steps, 3)),
-            dma((n,)), dma((n,)), dma((n,)), dma((n,)),
-        ],
-        compiler_params=params(0),
-        name="intersections",
-    )(slots, coefficients, domain)
-
-    def iterate(first, start):
-        shape = (quarter, width, width) if first else (pc, width, width)
+    big = (width, width)
+    x_shape = jax.ShapeDtypeStruct((n, quarter, *big), BF16)
+    block_scratch = [
+        pltpu.VMEM((n, pc, rows, width), BF16),
+        pltpu.VMEM((n, pc, rows), jnp.int32),
+        pltpu.VMEM((pc, width, NB), BF16),
+        pltpu.VMEM((pc, NB, width), BF16),
+        pltpu.VMEM((2, 2 * quarter, *big), F32),
+        pltpu.VMEM((2, 2 * quarter, *big), F32),
+        pltpu.VMEM((n, 2 * quarter, *big), F32),
+        pltpu.VMEM((2, quarter, *big), F32),
+        pltpu.VMEM((n, quarter, *big), F32),
+        pltpu.VMEM((n, quarter, *big), F32),
+        dma((2, steps, 3)), dma((2, steps, 3)),
+        dma((n,)), dma((n,)), dma((n,)), dma((n,)),
+    ]
+    amp_scratch = [
+        pltpu.VMEM((n * pc, *big), BF16),
+        pltpu.VMEM((pc, *big), BF16),
+        pltpu.VMEM((quarter, *big), F32),
+        pltpu.VMEM((quarter, *big), BF16),
+        dma((2, steps, 4)), dma((2, steps, 4)),
+        dma((n, 4)), dma((n, 4)), dma((n + 1,)), dma((n + 1,)), dma((3,)), dma((3,)),
+    ]
+    half_shape = jax.ShapeDtypeStruct((quarter, *big), BF16)
+
+    def iterate(first, start, x):
         return pl.pallas_call(
-            functools.partial(iteration, n, first),
-            out_shape=jax.ShapeDtypeStruct(shape, BF16),
+            functools.partial(iteration_alone, n, first),
+            out_shape=half_shape if first else jax.ShapeDtypeStruct((pc, *big), BF16),
             in_specs=[smem, smem, vmem, vmem, vmem, vmem],
             out_specs=vmem,
-            scratch_shapes=[
-                pltpu.VMEM((n * pc, width, width), BF16),
-                pltpu.VMEM((pc, width, width), BF16),
-                pltpu.VMEM((quarter, width, width), F32),
-                pltpu.VMEM((quarter, width, width), BF16),
-                dma((2, steps, 3)), dma((2, steps, 3)),
-                dma((n, 4)), dma((n, 4)), dma((n + 1,)), dma((n + 1,)), dma((3,)), dma((3,)),
-            ],
+            scratch_shapes=amp_scratch,
             compiler_params=params(1 if first else 2),
             name="first" if first else "second",
         )(slots, focks, start, x, exchange_integrals, pno_energy)
 
-    return iterate(False, iterate(True, amplitudes_start)).astype(F32)
+    held = n * width * (2 * pc * (rows + width) + 4 * width * 4 * quarter + 2 * width * quarter)
+    if held < 40 * 2**20:
+        x, amps = pl.pallas_call(
+            functools.partial(opening, n, len(block_scratch)),
+            out_shape=(x_shape, half_shape),
+            in_specs=[smem, smem, vmem, vmem, vmem, vmem, vmem],
+            out_specs=(vmem, vmem),
+            scratch_shapes=block_scratch + amp_scratch,
+            compiler_params=params(0),
+            name="opening",
+        )(slots, focks, coefficients, domain, amplitudes_start, exchange_integrals, pno_energy)
+    else:
+        x = pl.pallas_call(
+            functools.partial(intersections_alone, n),
+            out_shape=x_shape,
+            in_specs=[smem, vmem, vmem],
+            out_specs=vmem,
+            scratch_shapes=block_scratch,
+            compiler_params=params(0),
+            name="intersections",
+        )(slots, coefficients, domain)
+        amps = iterate(True, amplitudes_start, x)
+    return iterate(False, amps, x).astype(F32)
 
 
 def solution(mesh):

time: 132 us -> 115 us (0.87)
  Pallas kernels: 126 us -> 110 us
    pallas_call x3 -> x2, Pallas kernels: 126 us -> 110 us  [the longest x1 76.7 us: on_device(): pl.pallas_call(functools.partial(opening, n, len(block_scratch)), out_sha...]
where the time goes in v3:
time: 115 us
  Pallas kernels  110 us (96%)
  other arithmetic  3.52 us (3%)
  local copies, waits for them, and re-layouts  1.42 us (1%)
    pallas_call x1, Pallas kernels, on_device(): pl.pallas_call(functools.partial(opening, n, len(block_scratch)), out_sha...  76.7 us
    pallas_call x1, Pallas kernels, iterate(): pl.pallas_call(functools.partial(iteration_alone, n, first), out_shape=ha...  33.4 us

profile of v3, /device:TPU:0, one launch (start us, length us, event | category | flops | bytes accessed | tf_op | source)
XLA Modules:
  0.0 115.0 jit_solution(18123057581107879632)
XLA Ops:
  0.0 0.7 select_reduce_fusion.1
  0.7 0.0 copy-start
  0.7 0.0 copy-start.1
  0.7 0.7 copy.17.slot_ref.args_0_
  1.4 0.0 copy-done
  1.4 0.0 copy-done.1
  1.4 0.0 copy-start.2
  1.4 0.1 copy.14
  1.5 0.6 copy-done.2
  2.1 0.1 copy.15
  2.2 0.7 pad_maximum_fusion.fock_ref.args_1_
  2.9 76.7 %opening.1 = (bf16[8,4,128,128]{3,2,1,0:T(8,128)(2,1)}, bf16[4,128,128]{2,1,0:T(8,128)(2,1)}) custom-call(s32[16,8]{1,0:T(8,128)} %copy.17.slot_ref.args_0_, f32[16,9]{1,0:T(8,128)} %pad_maximum_fusion.fock_ref.args_1_, bf16[16,128,128]{2,1,0:T(8,128)(2,1)} %c_ref.1, s32[16,128]{1,0:T(8,128)} %dom_ref.1, f32[16,128,128]{2,1,0:T(8,128)} %start_ref.1, ...), custom_call_target="tpu_custom_call" | custom-call | tf_op jit(solution)/shard_map/opening/pallas_call | solution.py:534
  79.6 33.4 %second.1 = bf16[16,128,128]{2,1,0:T(8,128)(2,1)} custom-call(s32[16,8]{1,0:T(8,128)} %copy.17.slot_ref.args_0_, f32[16,9]{1,0:T(8,128)} %pad_maximum_fusion.fock_ref.args_1_, bf16[4,128,128]{2,1,0:T(8,128)(2,1)} %get-tuple-element.7.args_2_, bf16[8,4,128,128]{3,2,1,0:T(8,128)(2,1)} %get-tuple-element.8.args_3_, f32[16,128,128]{2,1,0:T(8,128)} %args_4_.4, ...), custom_call_target="tpu_custom_call" | custom-call | tf_op jit(solution)/shard_map/second/pallas_call | solution.py:522
  112.9 2.1 %convert_element_type.3 = f32[16,128,128]{2,1,0:T(8,128)} convert(bf16[16,128,128]{2,1,0:T(8,128)(2,1)} %second.1) | non-fusion elementwise | flops 262144 | bytes 1572864 | tf_op jit(solution)/shard_map/convert_element_type | solution.py:554
  (1 shorter events, 0.0 us)
Async XLA Ops:
  0.7 0.7 copy-start
  0.7 0.7 copy-start.1
  1.4 0.7 copy-start.2

commit v4 on v3

--- a/solution.py
+++ b/solution.py
@@ -220,7 +220,7 @@
 
 
 def iteration(
-    n, first, joined, slot_ref, fock_ref, start_ref, x_ref, k_ref, e_ref, out_ref,
+    n, first, joined, alone, slot_ref, fock_ref, start_ref, x_ref, k_ref, e_ref, out_ref,
     abuf, stage, acc, mine, rs, rr, ms, mr, ys, yr, fs, fr,
 ):
     p, g, position, mate, across = places(n)
@@ -231,7 +231,7 @@
     steps = n // 2
     right, left = at(position + 1, n), at(position - 1, n)
     diagonal = 3 - g
-    if not joined:
+    if alone:
         greet([(right, g), (left, g), (p, mate), (p, across)])
     parts = 4 if joined else 3
     parts_of = ring_parts(steps, parts)
@@ -447,7 +447,7 @@
 
 
 def iteration_alone(n, first, *args):
-    steps = iteration(n, first, False, *args)
+    steps = iteration(n, first, False, True, *args)
     next(steps)
     try:
         steps.send(None)
@@ -456,17 +456,29 @@
 
 
 def opening(
-    n, made, slot_ref, fock_ref, c_ref, dom_ref, start_ref, k_ref, e_ref, x_ref, out_ref, *scratch
+    n, made, slot_ref, fock_ref, c_ref, dom_ref, start_ref, k_ref, e_ref, out_ref,
+    x_ref, amp_ref, *scratch
 ):
+    used = made + (len(scratch) - made) // 2
     blocks = intersections(n, slot_ref, c_ref, dom_ref, x_ref, *scratch[:made])
     next(blocks)
     amps = iteration(
-        n, True, True, slot_ref, fock_ref, start_ref, x_ref, k_ref, e_ref, out_ref, *scratch[made:]
+        n, True, True, False, slot_ref, fock_ref, start_ref, x_ref, k_ref, e_ref, amp_ref,
+        *scratch[made:used],
     )
     next(amps)
     settle = next(blocks)
     try:
         amps.send(settle)
+    except StopIteration:
+        pass
+    amps = iteration(
+        n, False, False, False, slot_ref, fock_ref, amp_ref, x_ref, k_ref, e_ref, out_ref,
+        *scratch[used:],
+    )
+    next(amps)
+    try:
+        amps.send(None)
     except StopIteration:
         pass
     next(blocks, None)
@@ -531,15 +543,18 @@
 
     held = n * width * (2 * pc * (rows + width) + 4 * width * 4 * quarter + 2 * width * quarter)
     if held < 40 * 2**20:
-        x, amps = pl.pallas_call(
+        return pl.pallas_call(
             functools.partial(opening, n, len(block_scratch)),
-            out_shape=(x_shape, half_shape),
+            out_shape=jax.ShapeDtypeStruct((pc, *big), BF16),
             in_specs=[smem, smem, vmem, vmem, vmem, vmem, vmem],
-            out_specs=(vmem, vmem),
-            scratch_shapes=block_scratch + amp_scratch,
+            out_specs=vmem,
+            scratch_shapes=[
+                pltpu.VMEM(x_shape.shape, BF16), pltpu.VMEM(half_shape.shape, BF16),
+                *block_scratch, *amp_scratch, *amp_scratch,
+            ],
             compiler_params=params(0),
-            name="opening",
-        )(slots, focks, coefficients, domain, amplitudes_start, exchange_integrals, pno_energy)
+            name="amplitudes",
+        )(slots, focks, coefficients, domain, amplitudes_start, exchange_integrals, pno_energy).astype(F32)
     else:
         x = pl.pallas_call(
             functools.partial(intersections_alone, n),

time: 115 us -> 112 us (0.974)
  Pallas kernels: 110 us -> 107 us
    pallas_call x1 -> x0, Pallas kernels: 33.4 us -> none  [iterate(): pl.pallas_call(functools.partial(iteration_alone, n, first), out_shape=ha...]
    pallas_call x1, Pallas kernels: 76.7 us -> 107 us  [on_device(): pl.pallas_call(functools.partial(opening, n, len(block_scratch)), out_sha...]
where the time goes in v4:
time: 112 us
  Pallas kernels  107 us (96%)
  other arithmetic  3.52 us (3%)
  local copies, waits for them, and re-layouts  1.42 us (1%)
    pallas_call x1, Pallas kernels, on_device(): pl.pallas_call(functools.partial(opening, n, len(block_scratch)), out_sha...  107 us

profile of v4, /device:TPU:0, one launch (start us, length us, event | category | flops | bytes accessed | tf_op | source)
XLA Modules:
  0.0 111.7 jit_solution(3240286529966865701)
XLA Ops:
  0.0 0.7 select_reduce_fusion.1
  0.7 0.0 copy-start
  0.7 0.0 copy-start.1
  0.7 0.7 copy.16.slot_ref
  1.4 0.0 copy-done
  1.4 0.0 copy-done.1
  1.4 0.0 copy-start.2
  1.4 0.1 copy.14
  1.5 0.6 copy-done.2
  2.1 0.1 copy.15
  2.2 0.7 pad_maximum_fusion.fock_ref
  2.8 106.7 %amplitudes.1 = bf16[16,128,128]{2,1,0:T(8,128)(2,1)} custom-call(s32[16,8]{1,0:T(8,128)} %copy.16.slot_ref, f32[16,9]{1,0:T(8,128)} %pad_maximum_fusion.fock_ref, bf16[16,128,128]{2,1,0:T(8,128)(2,1)} %c_ref.1, s32[16,128]{1,0:T(8,128)} %dom_ref.1, f32[16,128,128]{2,1,0:T(8,128)} %start_ref.1, f32[16,128,128]{2,1,0:T(8,128)} %k_ref.1, f32[16,128]{1,0:T(8,128)} %e_ref.1), custom_call_target="tpu_custom_call" | custom-call | tf_op jit(solution)/shard_map/amplitudes/pallas_call | solution.py:546
  109.5 2.1 %convert_element_type.3 = f32[16,128,128]{2,1,0:T(8,128)} convert(bf16[16,128,128]{2,1,0:T(8,128)(2,1)} %amplitudes.1) | non-fusion elementwise | flops 262144 | bytes 1572864 | tf_op jit(solution)/shard_map/convert_element_type | solution.py:557
  (1 shorter events, 0.0 us)
Async XLA Ops:
  0.7 0.7 copy-start
  0.7 0.7 copy-start.1
  1.4 0.7 copy-start.2
